TPU v7x, 32 devices: a whole 2x2x4 slice. The times are simulated.
32 devices in a mesh: bond: 8 (over z, x), mpo: 4 (over y, core).
Axes of the slice: x: 2, y: 2, z: 4, core: 2. Of those that a mesh axis runs over, the one named last changes fastest.
Arguments:
- wave_blocks: bfloat16 [8, 16, 256, 256], P('bond'), may hold values from -6 to 6
- left_environment: bfloat16 [8, 8, 256, 256], P('mpo', 'bond'), may hold values from -0.375 to 0.375
- right_environment: bfloat16 [8, 8, 256, 256], P('mpo', 'bond'), may hold values from -0.375 to 0.375
- site_operators: bfloat16 [8, 16, 16], P('mpo'), may hold values from -1.1953125 to 1.1953125
- right_sector: int32 [8, 16, 1], P('bond'), may hold values from 0 to 7; in each aligned block of 16 rows (0 to 15, 16 to 31, ..., all dimensions but the last counted through in order) at most 2 rows name the same one
- left_sizes: int32 [8], replicated, may hold values from 128 to 256
- right_sizes: int32 [8], replicated, may hold values from 128 to 256
- sector_place: int32 [8], replicated, may hold values from 0 to 7, each once
Outputs:
- applied: bfloat16 [8, 16, 256, 256], P('bond', 'mpo')
Inputs may be any that keep to these rules, and one draw needn't show every extreme that they name: `right_sector`: among the 16 blocks of one bond index no right sector is named more than 2 times, a bound that some block reaches. `sector_place`: every position is taken by exactly one right sector.
All inputs are finite; a program needn't handle non-finite values.
Results may differ from a plain program's by a relative error of at most 0.0057.
Values may be sent and summed in bfloat16 or wider, within the bound.
A program may use at most 64 MiB of HBM per device.

v0:
```python
import jax
import jax.numpy as jnp
from jax import lax
from jax.sharding import PartitionSpec as P


def lookup(entries, indices):
    count = entries.shape[0]
    matches = indices[..., None] == jnp.arange(count, dtype=jnp.int32)
    return jnp.sum(jnp.where(matches, entries, 0), axis=-1)


def shards(
    wave_blocks,
    left_environment,
    right_environment,
    site_operators,
    right_sector,
    left_sizes,
    right_sizes,
    sector_place,
):
    sectors = wave_blocks.shape[0]
    states = wave_blocks.shape[1]
    block_rows = wave_blocks.shape[2]
    channels = left_environment.shape[0]
    first_sector = lax.axis_index("bond") * sectors
    sector_ids = right_sector[:, :, 0]
    offsets = jnp.arange(block_rows, dtype=jnp.int32)
    left_live = lax.dynamic_slice_in_dim(left_sizes, first_sector, sectors)
    row_mask = offsets[None, :] < left_live[:, None]
    column_mask = offsets[None, None, :] < lookup(right_sizes, sector_ids)[:, :, None]
    live_mask = row_mask[:, None, :, None] & column_mask[:, :, None, :]
    masked = jnp.where(live_mask, wave_blocks, jnp.zeros((), jnp.bfloat16))
    block_count = sectors * states
    flat_blocks = masked.reshape(block_count, block_rows, block_rows)
    place_flat = lookup(sector_place, sector_ids).reshape(block_count)
    gathered = lax.all_gather(right_environment, "bond", axis=1, tiled=True)
    chosen = jnp.take(gathered, place_flat, axis=1)
    right_part = jnp.einsum(
        "bac,hbxc->bhax", flat_blocks, chosen, preferred_element_type=jnp.float32
    ).astype(jnp.bfloat16)
    right_part = right_part.reshape(sectors, states, channels, block_rows, block_rows)
    same_sector = sector_ids[:, :, None] == sector_ids[:, None, :]
    mixing = jnp.where(same_sector[:, None], site_operators[None], jnp.zeros((), jnp.bfloat16))
    mixed = jnp.einsum(
        "nhst,nthac->nshac", mixing, right_part, preferred_element_type=jnp.float32
    ).astype(jnp.bfloat16)
    partial_value = jnp.einsum(
        "hnab,nshbc->nsac", left_environment, mixed, preferred_element_type=jnp.float32
    )
    per_device = states // lax.axis_size("mpo")
    first_state = lax.axis_index("mpo") * per_device
    summed = lax.psum(partial_value, "mpo")
    summed = lax.dynamic_slice_in_dim(summed, first_state, per_device, 1)
    kept_mask = lax.dynamic_slice_in_dim(live_mask, first_state, per_device, 1)
    return jnp.where(kept_mask, summed, jnp.zeros((), jnp.float32)).astype(jnp.bfloat16)


def solution(mesh):
    placed = (
        P("bond", None, None, None),
        P("mpo", "bond", None, None),
        P("mpo", "bond", None, None),
        P("mpo", None, None),
        P("bond", None, None),
        P(),
        P(),
        P(),
    )
    return jax.shard_map(
        shards, mesh=mesh, in_specs=placed, out_specs=P("bond", "mpo", None, None), check_vma=False
    )
```

profile of v0, /device:TPU:0, one launch (start us, length us, event | category | flops | bytes accessed | tf_op | source)
XLA Modules:
  0.0 172.7 jit_solution(5104987714782508854)
XLA Ops:
  6.5 0.0 copy-start
  6.5 0.0 copy-start.5
  6.5 0.0 copy-start.2
  6.5 0.0 copy-start.3
  6.5 0.0 copy-start.4
  6.5 0.0 all-gather.2.cloned.1.call-start
  6.6 0.7 all-gather.2.cloned.1.call-update
  7.3 2.9 %copy.12 = bf16[1,16,256,256]{2,3,1,0:T(8,128)(2,1)S(1)} copy(bf16[1,16,256,256]{3,2,1,0:T(8,128)(2,1)} %param.8) | data formatting | bytes 4194304 | tf_op args[0]
  10.2 0.0 copy-done.5
  10.2 0.6 dynamic_slice.9
  10.8 0.6 iota_compare_fusion.2
  11.4 0.0 copy-done.2
  11.4 0.0 copy-done.3
  11.4 0.0 copy-done.4
  11.4 0.1 select_reduce_fusion.1
  11.6 0.1 broadcast_compare_fusion
  11.6 0.1 iota_compare_fusion
  11.7 2.0 %broadcast_and_fusion = pred[1,16,256,256]{2,3,1,0:T(8,128)(4,1)} fusion(pred[16,256]{1,0:T(8,128)(4,1)S(1)} %iota_compare_fusion, pred[256]{0:T(512)(128)(4,1)S(1)} %iota_compare_fusion.2), kind=kLoop, calls=%fused_computation.15 | loop fusion | flops 1048576 | bytes 1052928 | tf_op jit(solution)/shard_map/and | solution.py:33
  13.7 47.6 %all-gather.2.cloned.1.call-done = bf16[2,8,256,256]{3,2,1,0:T(8,128)(2,1)} async-done(((bf16[2,1,256,256]{3,2,1,0:T(8,128)(2,1)}), bf16[2,8,256,256]{3,2,1,0:T(8,128)(2,1)}) %all-gather.2.cloned.1.call-update) | async-done | bytes 2097168 | tf_op jit(solution)/shard_map/all_gather | solution.py:38
  61.4 4.3 %gather_fusion = bf16[16,2,256,256]{3,2,1,0:T(8,128)(2,1)} fusion(bf16[2,8,256,256]{3,2,1,0:T(8,128)(2,1)} %all-gather.2.cloned.1.call-done, s32[1024]{0:T(1024)S(1)} %pad_clamp_fusion), kind=kCustom, calls=%fused_computation | custom fusion | bytes 8388672 | tf_op jit(solution)/shard_map/jit(_take)/gather | solution.py:39
  65.7 4.7 %fusion.2 = bf16[16,2,256,256]{3,2,1,0:T(8,128)(2,1)} fusion(bf16[16,2,256,256]{3,2,1,0:T(8,128)(2,1)} %gather_fusion, pred[16]{0:T(512)(128)(4,1)S(1)} %compare_and_fusion, bf16[1,16,256,256]{2,3,1,0:T(8,128)(2,1)S(1)} %copy.12, pred[16,256]{1,0:T(8,128)(4,1)S(1)} %iota_compare_fusion, pred[256]{0:T(512)(128)(4,1)S(1)} %iota_compare_fusion.2), kind=kOutput, calls=%fused_computation.3 | convolution fusion | flops 1077936128 | bytes 10490128 | tf_op jit(solution)/shard_map/bac,hbxc->bhax/dot_general | solution.py:40
  70.4 0.0 copy-start.1
  70.4 7.9 %copy.16 = bf16[16,2,256,256]{2,0,3,1:T(8,128)(2,1)} copy(bf16[16,2,256,256]{3,2,1,0:T(8,128)(2,1)} %fusion.2) | data formatting | bytes 8388608 | tf_op jit(solution)/shard_map/bac,hbxc->bhax/dot_general | solution.py:40
  78.3 0.0 copy-done.1
  78.3 3.4 %convert_bitcast_fusion = bf16[16,2,256,256]{3,0,2,1:T(8,128)(2,1)S(1)} fusion(bf16[16,2,256,256]{2,0,3,1:T(8,128)(2,1)} %copy.16, bf16[2,16,16]{2,1,0:T(8,128)(2,1)S(1)} %copy-done.1, pred[16,16]{1,0:T(8,128)(4,1)S(1)} %broadcast_compare_fusion), kind=kOutput, calls=%fused_computation.8 | convolution fusion | flops 69206528 | bytes 8389888 | tf_op jit(solution)/shard_map/nhst,nthac->nshac/dot_general | solution.py:46
  81.7 0.0 copy-done
  81.7 6.1 %fusion.11 = f32[1,16,256,256]{2,3,1,0:T(8,128)} fusion(bf16[16,2,256,256]{3,0,2,1:T(8,128)(2,1)S(1)} %convert_bitcast_fusion, bf16[2,1,256,256]{3,2,1,0:T(8,128)(2,1)S(1)} %copy-done), kind=kOutput, calls=%fused_computation.11 | convolution fusion | flops 1073741824 | bytes 8650752 | tf_op jit(solution)/shard_map/hnab,nshbc->nsac/dot_general | solution.py:49
  87.8 75.9 %all-reduce.1 = bf16[1,16,256,256]{2,3,1,0:T(8,128)(2,1)S(1)} all-reduce(f32[1,16,256,256]{2,3,1,0:T(8,128)} %fusion.11), channel_id=1, replica_groups=mesh['bond'=8,'mpo'=4] {'mpo'}, use_global_device_ids=true, to_apply=%region_2.3 | all-reduce | flops 1048576 | bytes 6291456 | tf_op jit(solution)/shard_map/psum | solution.py:54
  163.7 1.1 select_convert_fusion
  164.8 1.0 copy.14
  (3 shorter events, 0.0 us)
Async XLA Ops:
  6.5 75.1 %copy-start = (bf16[2,1,256,256]{3,2,1,0:T(8,128)(2,1)S(1)}, bf16[2,1,256,256]{3,2,1,0:T(8,128)(2,1)}, u32[]{:S(2)}) copy-start(bf16[2,1,256,256]{3,2,1,0:T(8,128)(2,1)} %param.9) | copy-start | bytes 786436
  6.5 3.6 %copy-start.5 = (s32[8]{0:T(128)S(1)}, s32[8]{0:T(128)}, u32[]{:S(2)}) copy-start(s32[8]{0:T(128)} %param.13) | copy-start | bytes 100
  6.5 4.9 %copy-start.2 = (s32[1,16,1]{1,2,0:T(1,128)S(1)}, s32[1,16,1]{1,2,0:T(1,128)}, u32[]{:S(2)}) copy-start(s32[1,16,1]{1,2,0:T(1,128)} %param.12) | copy-start | bytes 196
  6.5 4.9 %copy-start.3 = (s32[8]{0:T(128)S(1)}, s32[8]{0:T(128)}, u32[]{:S(2)}) copy-start(s32[8]{0:T(128)} %param.14) | copy-start | bytes 100
  6.5 4.9 %copy-start.4 = (s32[8]{0:T(128)S(1)}, s32[8]{0:T(128)}, u32[]{:S(2)}) copy-start(s32[8]{0:T(128)} %param.15) | copy-start | bytes 100
  6.5 54.8 %all-gather.2.cloned.1.call-start = ((), (), s32[]{:S(2)}) async-start(), calls=%async_computation | async-start | bytes 2359296 | tf_op jit(solution)/shard_map/all_gather | solution.py:38
  70.4 7.9 %copy-start.1 = (bf16[2,16,16]{2,1,0:T(8,128)(2,1)S(1)}, bf16[2,16,16]{2,1,0:T(8,128)(2,1)}, u32[]{:S(2)}) copy-start(bf16[2,16,16]{2,1,0:T(8,128)(2,1)} %param.11) | copy-start | bytes 3076
Sparse Core Ops, SparseCore 0:
  9.5 51.7 all-gather.1
where the time goes:
time: 173 us
  blocking collectives  75.9 us (44%)
  waiting for transfers between devices  48.3 us (28%)
  local copies, waits for them, and re-layouts  16.7 us (10%)
  matrix products  14.2 us (8%)
  between operations  13.5 us (8%)
  other arithmetic  4.04 us (2%)
    psum x1, blocking collectives, shards(): summed = lax.psum(partial_value, 'mpo')  75.9 us
    all_gather x1, waiting for transfers between devices, shards(): gathered = lax.all_gather(right_environment, 'bond', axis=1, tiled=True)  47.6 us
    dot_general x1, local copies, waits for them, and re-layouts, shards(): jnp.einsum('bac,hbxc->bhax', flat_blocks, chosen, preferred_element_type=...  7.89 us
    dot_general x1, matrix products, shards(): jnp.einsum('hnab,nshbc->nsac', left_environment, mixed, preferred_element...  6.13 us
    dot_general x1, matrix products, shards(): jnp.einsum('bac,hbxc->bhax', flat_blocks, chosen, preferred_element_type=...  4.66 us
    gather x1, local copies, waits for them, and re-layouts, shards(): chosen = jnp.take(gathered, place_flat, axis=1)  4.34 us
  transfers between devices with their start and end apart: 1, of which 1 were waited for; matrix products, arithmetic and copies ran while one was open for 4% of the time, Pallas kernels for 0%

commit v1 on v0

--- a/solution.py
+++ b/solution.py
@@ -2,6 +2,28 @@
 import jax.numpy as jnp
 from jax import lax
 from jax.sharding import PartitionSpec as P
+
+
+def joined_along(pieces, dim):
+    lengths = list(pieces.shape[1:])
+    lengths[dim] *= pieces.shape[0]
+    return jnp.moveaxis(pieces, 0, dim).reshape(lengths)
+
+
+def gather_around(x, axis, dim):
+    size = lax.axis_size(axis)
+    pairs = [(i, (i + 1) % size) for i in range(size)]
+    back = [(b, a) for a, b in pairs]
+    lower, upper = ([], [])
+    for lap in range(size - 1):
+        if lap % 2 == 0:
+            lower.append(lax.ppermute(lower[-1] if lower else x, axis, pairs))
+        else:
+            upper.append(lax.ppermute(upper[-1] if upper else x, axis, back))
+    pieces = jnp.stack([*lower[::-1], x, *upper])
+    shift = lax.axis_index(axis) - len(lower)
+    pieces = pieces[(jnp.arange(size) - shift) % size]
+    return joined_along(pieces, dim)
 
 
 def lookup(entries, indices):
@@ -35,7 +57,7 @@
     block_count = sectors * states
     flat_blocks = masked.reshape(block_count, block_rows, block_rows)
     place_flat = lookup(sector_place, sector_ids).reshape(block_count)
-    gathered = lax.all_gather(right_environment, "bond", axis=1, tiled=True)
+    gathered = gather_around(right_environment, "bond", 1)
     chosen = jnp.take(gathered, place_flat, axis=1)
     right_part = jnp.einsum(
         "bac,hbxc->bhax", flat_blocks, chosen, preferred_element_type=jnp.float32

time: 173 us -> 163 us (0.942)
  waiting for transfers between devices: 48.3 us -> 28.5 us
  starting transfers between devices: 0.04 us -> 15.8 us
  between operations: 13.5 us -> 0.14 us
  local copies, waits for them, and re-layouts: 16.7 us -> 20.6 us
    all_gather x1 -> x0, waiting for transfers between devices: 47.6 us -> none  [shards(): gathered = lax.all_gather(right_environment, 'bond', axis=1, tiled=True)]
    ppermute x0 -> x7, waiting for transfers between devices: none -> 28.5 us  [the longest x4 14.9 us: gather_around(): lower.append(lax.ppermute(lower[-1] if lower else x, axis, pairs))]
    ppermute x0 -> x7, starting transfers between devices: none -> 15.8 us  [the longest x4 7.97 us: gather_around(): lower.append(lax.ppermute(lower[-1] if lower else x, axis, pairs))]
    unnamed x13 -> x16, local copies, waits for them, and re-layouts: 2.88 us -> 5.37 us
    gather x0 -> x1, local copies, waits for them, and re-layouts: none -> 2.27 us  [gather_around(): pieces = pieces[(jnp.arange(size) - shift) % size]]
  transfers between devices with their start and end apart: 1 -> 7, of which waited for: 1 -> 5; matrix products, arithmetic and copies ran while one was open for 4% -> 6% of each run, Pallas kernels for 0% -> 0%
where the time goes in v1:
time: 163 us; the launch traced here: 162 us
  blocking collectives  75.8 us (47%)
  waiting for transfers between devices  28.5 us (17%)
  local copies, waits for them, and re-layouts  20.6 us (13%)
  starting transfers between devices  15.8 us (10%)
  matrix products  15.8 us (10%)
  other arithmetic  5.49 us (3%)
    psum x1, blocking collectives, shards(): summed = lax.psum(partial_value, 'mpo')  75.8 us
    ppermute x4, waiting for transfers between devices, gather_around(): lower.append(lax.ppermute(lower[-1] if lower else x, axis, pairs))  14.9 us
    ppermute x3, waiting for transfers between devices, gather_around(): upper.append(lax.ppermute(upper[-1] if upper else x, axis, back))  13.7 us
    ppermute x4, starting transfers between devices, gather_around(): lower.append(lax.ppermute(lower[-1] if lower else x, axis, pairs))  7.97 us
    dot_general x1, local copies, waits for them, and re-layouts, shards(): jnp.einsum('bac,hbxc->bhax', flat_blocks, chosen, preferred_element_type=...  7.92 us
    ppermute x3, starting transfers between devices, gather_around(): upper.append(lax.ppermute(upper[-1] if upper else x, axis, back))  7.84 us
    dot_general x1, matrix products, shards(): jnp.einsum('bac,hbxc->bhax', flat_blocks, chosen, preferred_element_type=...  6.24 us
    dot_general x1, matrix products, shards(): jnp.einsum('hnab,nshbc->nsac', left_environment, mixed, preferred_element...  6.13 us
  transfers between devices with their start and end apart: 7, of which 5 were waited for; matrix products, arithmetic and copies ran while one was open for 6% of the time, Pallas kernels for 0%

profile of v1, /device:TPU:0, one launch (start us, length us, event | category | flops | bytes accessed | tf_op | source)
XLA Modules:
  0.0 162.2 jit_solution(12574402560268231379)
XLA Ops:
  0.0 0.0 copy-start
  0.0 3.0 %collective-permute-start = (bf16[2,1,256,256]{3,2,1,0:T(8,128)(2,1)}, bf16[2,1,256,256]{3,2,1,0:T(8,128)(2,1)S(1)}, u32[]{:S(2)}, u32[]{:S(2)}) collective-permute-start(bf16[2,1,256,256]{3,2,1,0:T(8,128)(2,1)} %param.10), channel_id=1, source_target_pairs={{0,4},{4,8},{8,12},{12,16},{16,20},{20,24},{24,28},{28,0},{1,5},{5... | collective-permute-start | bytes 786440 | tf_op jit(solution)/shard_map/ppermute | solution.py:20
  3.0 3.1 %collective-permute-start.4 = (bf16[2,1,256,256]{3,2,0,1:T(8,128)(2,1)}, bf16[2,1,256,256]{3,2,0,1:T(8,128)(2,1)S(1)}, u32[]{:S(2)}, u32[]{:S(2)}) collective-permute-start(bf16[2,1,256,256]{3,2,0,1:T(8,128)(2,1)} %bitcast.69), channel_id=1, source_target_pairs={{4,0},{8,4},{12,8},{16,12},{20,16},{24,20},{28,24},{0,28},{5,1},{9... | collective-permute-start | bytes 786440 | tf_op jit(solution)/shard_map/ppermute | solution.py:22
  6.1 0.8 select_reduce_fusion.1
  6.9 7.6 %collective-permute-done = bf16[2,1,256,256]{3,2,1,0:T(8,128)(2,1)S(1)} collective-permute-done((bf16[2,1,256,256]{3,2,1,0:T(8,128)(2,1)}, bf16[2,1,256,256]{3,2,1,0:T(8,128)(2,1)S(1)}, u32[]{:S(2)}, u32[]{:S(2)}) %collective-permute-start) | collective-permute-done | bytes 262176 | tf_op jit(solution)/shard_map/ppermute | solution.py:20
  14.5 2.4 %collective-permute-start.1 = (bf16[2,1,256,256]{3,2,0,1:T(8,128)(2,1)S(1)}, bf16[2,1,256,256]{3,2,0,1:T(8,128)(2,1)S(1)}, u32[]{:S(2)}, u32[]{:S(2)}) collective-permute-start(bf16[2,1,256,256]{3,2,0,1:T(8,128)(2,1)S(1)} %bitcast.70), channel_id=1, source_target_pairs={{0,4},{4,8},{8,12},{12,16},{16,20},{20,24},{24,28},{28,0},{1,5},{5... | collective-permute-start | bytes 786440 | tf_op jit(solution)/shard_map/ppermute | solution.py:20
  16.9 1.2 dynamic_slice.9
  18.1 0.8 broadcast_compare_fusion
  18.9 6.4 %collective-permute-done.1 = bf16[2,1,256,256]{3,2,0,1:T(8,128)(2,1)S(1)} collective-permute-done((bf16[2,1,256,256]{3,2,0,1:T(8,128)(2,1)S(1)}, bf16[2,1,256,256]{3,2,0,1:T(8,128)(2,1)S(1)}, u32[]{:S(2)}, u32[]{:S(2)}) %collective-permute-start.1) | collective-permute-done | bytes 262176 | tf_op jit(solution)/shard_map/ppermute | solution.py:20
  25.3 0.0 collective-permute-start.2
  25.3 0.7 iota_compare_fusion.2
  26.0 3.9 %copy.16 = bf16[1,16,256,256]{2,3,1,0:T(8,128)(2,1)} copy(bf16[1,16,256,256]{3,2,1,0:T(8,128)(2,1)} %param.8) | data formatting | bytes 4194304 | tf_op args[0]
  29.9 0.0 copy-start.2
  29.9 0.1 iota_compare_fusion
  30.0 0.0 collective-permute-done.4
  30.0 4.7 %collective-permute-start.5 = (bf16[2,1,256,256]{3,2,0,1:T(8,128)(2,1)S(1)}, bf16[2,1,256,256]{3,2,0,1:T(8,128)(2,1)S(1)}, u32[]{:S(2)}, u32[]{:S(2)}) collective-permute-start(bf16[2,1,256,256]{3,2,0,1:T(8,128)(2,1)S(1)} %collective-permute-done.4), channel_id=1, source_target_pairs={{4,0},{8,4},{12,8},{16,12},{20,16},{24,20},{28,24},{0,28},{5,1},{9... | collective-permute-start | bytes 786440 | tf_op jit(solution)/shard_map/ppermute | solution.py:22
  34.7 0.8 collective-permute-done.2
  35.5 2.6 %collective-permute-start.3 = (bf16[2,1,256,256]{3,2,0,1:T(8,128)(2,1)S(1)}, bf16[2,1,256,256]{3,2,0,1:T(8,128)(2,1)S(1)}, u32[]{:S(2)}, u32[]{:S(2)}) collective-permute-start(bf16[2,1,256,256]{3,2,0,1:T(8,128)(2,1)S(1)} %collective-permute-done.2), channel_id=1, source_target_pairs={{0,4},{4,8},{8,12},{12,16},{16,20},{20,24},{24,28},{28,0},{1,5},{5... | collective-permute-start | bytes 786440 | tf_op jit(solution)/shard_map/ppermute | solution.py:20
  38.2 2.0 %broadcast_and_fusion = pred[1,16,256,256]{2,3,1,0:T(8,128)(4,1)} fusion(pred[16,256]{1,0:T(8,128)(4,1)S(1)} %iota_compare_fusion, pred[256]{0:T(512)(128)(4,1)S(1)} %iota_compare_fusion.2), kind=kLoop, calls=%fused_computation.16 | loop fusion | flops 1048576 | bytes 1052928 | tf_op jit(solution)/shard_map/and | solution.py:55
  40.2 5.7 %collective-permute-done.5 = bf16[2,1,256,256]{3,2,0,1:T(8,128)(2,1)S(1)} collective-permute-done((bf16[2,1,256,256]{3,2,0,1:T(8,128)(2,1)S(1)}, bf16[2,1,256,256]{3,2,0,1:T(8,128)(2,1)S(1)}, u32[]{:S(2)}, u32[]{:S(2)}) %collective-permute-start.5) | collective-permute-done | bytes 262176 | tf_op jit(solution)/shard_map/ppermute | solution.py:22
  45.9 0.0 collective-permute-start.6
  45.9 0.0 collective-permute-done.3
  46.0 0.0 copy-done.2
  46.1 8.0 %collective-permute-done.6 = bf16[2,1,256,256]{3,2,0,1:T(8,128)(2,1)S(1)} collective-permute-done((bf16[2,1,256,256]{3,2,0,1:T(8,128)(2,1)S(1)}, bf16[2,1,256,256]{3,2,0,1:T(8,128)(2,1)S(1)}, u32[]{:S(2)}, u32[]{:S(2)}) %collective-permute-start.6) | collective-permute-done | bytes 262176 | tf_op jit(solution)/shard_map/ppermute | solution.py:22
  54.1 0.0 copy-start.1
  54.1 1.3 copy-done.1
  55.5 2.3 %gather_fusion = bf16[8,2,256,256]{3,2,1,0:T(8,128)(2,1)S(1)} fusion(bf16[8,2,256,256]{3,2,1,0:T(8,128)(2,1)} %bitcast.68, s32[1024]{0:T(1024)S(1)} %pad_clamp_fusion.1), kind=kCustom, calls=%fused_computation | custom fusion | bytes 4194336 | tf_op jit(solution)/shard_map/gather | solution.py:25
  57.7 2.8 %gather_fusion.1 = bf16[16,2,256,256]{3,2,1,0:T(8,128)(2,1)} fusion(bf16[2,8,256,256]{3,2,0,1:T(8,128)(2,1)S(1)} %bitcast.67, s32[1024]{0:T(1024)S(1)} %pad_clamp_fusion), kind=kCustom, calls=%fused_computation.1 | custom fusion | bytes 8388672 | tf_op jit(solution)/shard_map/jit(_take)/gather | solution.py:61
  60.5 6.2 %fusion.2 = bf16[16,2,256,256]{3,2,1,0:T(8,128)(2,1)} fusion(bf16[16,2,256,256]{3,2,1,0:T(8,128)(2,1)} %gather_fusion.1, pred[16]{0:T(512)(128)(4,1)S(1)} %compare_and_fusion, bf16[1,16,256,256]{2,3,1,0:T(8,128)(2,1)} %copy.16, pred[16,256]{1,0:T(8,128)(4,1)S(1)} %iota_compare_fusion, pred[256]{0:T(512)(128)(4,1)S(1)} %iota_compare_fusion.2), kind=kOutput, calls=%fused_computation.4 | convolution fusion | flops 1077936128 | bytes 10490128 | tf_op jit(solution)/shard_map/bac,hbxc->bhax/dot_general | solution.py:62
  66.8 0.0 copy-start.3
  66.8 7.9 %copy.20 = bf16[16,2,256,256]{2,0,3,1:T(8,128)(2,1)} copy(bf16[16,2,256,256]{3,2,1,0:T(8,128)(2,1)} %fusion.2) | data formatting | bytes 8388608 | tf_op jit(solution)/shard_map/bac,hbxc->bhax/dot_general | solution.py:62
  74.7 0.0 copy-done.3
  74.7 3.4 %convert_bitcast_fusion = bf16[16,2,256,256]{3,0,2,1:T(8,128)(2,1)S(1)} fusion(bf16[16,2,256,256]{2,0,3,1:T(8,128)(2,1)} %copy.20, bf16[2,16,16]{2,1,0:T(8,128)(2,1)S(1)} %copy-done.3, pred[16,16]{1,0:T(8,128)(4,1)S(1)} %broadcast_compare_fusion), kind=kOutput, calls=%fused_computation.9 | convolution fusion | flops 69206528 | bytes 8389888 | tf_op jit(solution)/shard_map/nhst,nthac->nshac/dot_general | solution.py:68
  78.1 0.0 copy-done
  78.1 6.1 %fusion.11 = f32[1,16,256,256]{2,3,1,0:T(8,128)} fusion(bf16[16,2,256,256]{3,0,2,1:T(8,128)(2,1)S(1)} %convert_bitcast_fusion, bf16[2,1,256,256]{3,2,1,0:T(8,128)(2,1)S(1)} %copy-done), kind=kOutput, calls=%fused_computation.12 | convolution fusion | flops 1073741824 | bytes 8650752 | tf_op jit(solution)/shard_map/hnab,nshbc->nsac/dot_general | solution.py:71
  84.2 75.8 %all-reduce.1 = bf16[1,16,256,256]{2,3,1,0:T(8,128)(2,1)S(1)} all-reduce(f32[1,16,256,256]{2,3,1,0:T(8,128)} %fusion.11), channel_id=1, replica_groups=mesh['bond'=8,'mpo'=4] {'mpo'}, use_global_device_ids=true, to_apply=%region_2.3 | all-reduce | flops 1048576 | bytes 6291456 | tf_op jit(solution)/shard_map/psum | solution.py:76
  160.1 1.1 select_convert_fusion
  161.2 1.0 copy.18
  (13 shorter events, 0.2 us)
Async XLA Ops:
  0.0 78.1 %copy-start = (bf16[2,1,256,256]{3,2,1,0:T(8,128)(2,1)S(1)}, bf16[2,1,256,256]{3,2,1,0:T(8,128)(2,1)}, u32[]{:S(2)}) copy-start(bf16[2,1,256,256]{3,2,1,0:T(8,128)(2,1)} %param.9) | copy-start | bytes 786436
  0.0 14.5 %collective-permute-start = (bf16[2,1,256,256]{3,2,1,0:T(8,128)(2,1)}, bf16[2,1,256,256]{3,2,1,0:T(8,128)(2,1)S(1)}, u32[]{:S(2)}, u32[]{:S(2)}) collective-permute-start(bf16[2,1,256,256]{3,2,1,0:T(8,128)(2,1)} %param.10), channel_id=1, source_target_pairs={{0,4},{4,8},{8,12},{12,16},{16,20},{20,24},{24,28},{28,0},{1,5},{5... | collective-permute-start | bytes 786440 | tf_op jit(solution)/shard_map/ppermute | solution.py:20
  3.0 27.0 %collective-permute-start.4 = (bf16[2,1,256,256]{3,2,0,1:T(8,128)(2,1)}, bf16[2,1,256,256]{3,2,0,1:T(8,128)(2,1)S(1)}, u32[]{:S(2)}, u32[]{:S(2)}) collective-permute-start(bf16[2,1,256,256]{3,2,0,1:T(8,128)(2,1)} %bitcast.69), channel_id=1, source_target_pairs={{4,0},{8,4},{12,8},{16,12},{20,16},{24,20},{28,24},{0,28},{5,1},{9... | collective-permute-start | bytes 786440 | tf_op jit(solution)/shard_map/ppermute | solution.py:22
  14.5 10.9 %collective-permute-start.1 = (bf16[2,1,256,256]{3,2,0,1:T(8,128)(2,1)S(1)}, bf16[2,1,256,256]{3,2,0,1:T(8,128)(2,1)S(1)}, u32[]{:S(2)}, u32[]{:S(2)}) collective-permute-start(bf16[2,1,256,256]{3,2,0,1:T(8,128)(2,1)S(1)} %bitcast.70), channel_id=1, source_target_pairs={{0,4},{4,8},{8,12},{12,16},{16,20},{20,24},{24,28},{28,0},{1,5},{5... | collective-permute-start | bytes 786440 | tf_op jit(solution)/shard_map/ppermute | solution.py:20
  25.3 10.2 %collective-permute-start.2 = (bf16[2,1,256,256]{3,2,0,1:T(8,128)(2,1)S(1)}, bf16[2,1,256,256]{3,2,0,1:T(8,128)(2,1)S(1)}, u32[]{:S(2)}, u32[]{:S(2)}) collective-permute-start(bf16[2,1,256,256]{3,2,0,1:T(8,128)(2,1)S(1)} %collective-permute-done.1), channel_id=1, source_target_pairs={{0,4},{4,8},{8,12},{12,16},{16,20},{20,24},{24,28},{28,0},{1,5},{5... | collective-permute-start | bytes 786440 | tf_op jit(solution)/shard_map/ppermute | solution.py:20
  29.9 16.1 %copy-start.2 = (bf16[2,1,256,256]{3,2,1,0:T(8,128)(2,1)S(1)}, bf16[2,1,256,256]{3,2,1,0:T(8,128)(2,1)}, u32[]{:S(2)}) copy-start(bf16[2,1,256,256]{3,2,1,0:T(8,128)(2,1)} %param.10) | copy-start | bytes 786436
  30.0 15.9 %collective-permute-start.5 = (bf16[2,1,256,256]{3,2,0,1:T(8,128)(2,1)S(1)}, bf16[2,1,256,256]{3,2,0,1:T(8,128)(2,1)S(1)}, u32[]{:S(2)}, u32[]{:S(2)}) collective-permute-start(bf16[2,1,256,256]{3,2,0,1:T(8,128)(2,1)S(1)} %collective-permute-done.4), channel_id=1, source_target_pairs={{4,0},{8,4},{12,8},{16,12},{20,16},{24,20},{28,24},{0,28},{5,1},{9... | collective-permute-start | bytes 786440 | tf_op jit(solution)/shard_map/ppermute | solution.py:22
  35.5 10.3 %collective-permute-start.3 = (bf16[2,1,256,256]{3,2,0,1:T(8,128)(2,1)S(1)}, bf16[2,1,256,256]{3,2,0,1:T(8,128)(2,1)S(1)}, u32[]{:S(2)}, u32[]{:S(2)}) collective-permute-start(bf16[2,1,256,256]{3,2,0,1:T(8,128)(2,1)S(1)} %collective-permute-done.2), channel_id=1, source_target_pairs={{0,4},{4,8},{8,12},{12,16},{16,20},{20,24},{24,28},{28,0},{1,5},{5... | collective-permute-start | bytes 786440 | tf_op jit(solution)/shard_map/ppermute | solution.py:20
  45.9 8.2 %collective-permute-start.6 = (bf16[2,1,256,256]{3,2,0,1:T(8,128)(2,1)S(1)}, bf16[2,1,256,256]{3,2,0,1:T(8,128)(2,1)S(1)}, u32[]{:S(2)}, u32[]{:S(2)}) collective-permute-start(bf16[2,1,256,256]{3,2,0,1:T(8,128)(2,1)S(1)} %collective-permute-done.5), channel_id=1, source_target_pairs={{4,0},{8,4},{12,8},{16,12},{20,16},{24,20},{28,24},{0,28},{5,1},{9... | collective-permute-start | bytes 786440 | tf_op jit(solution)/shard_map/ppermute | solution.py:22
  54.1 1.3 copy-start.1
  66.8 7.9 %copy-start.3 = (bf16[2,16,16]{2,1,0:T(8,128)(2,1)S(1)}, bf16[2,16,16]{2,1,0:T(8,128)(2,1)}, u32[]{:S(2)}) copy-start(bf16[2,16,16]{2,1,0:T(8,128)(2,1)} %param.11) | copy-start | bytes 3076
